TPU v7x, 512 devices: a whole 4x8x8 slice. The times are simulated.
512 devices in a mesh: ctx: 64 (over y, z), ch: 8 (over x, core).
Axes of the slice: x: 4, y: 8, z: 8, core: 2. Of those that a mesh axis runs over, the one named last changes fastest.
Arguments:
- features: bfloat16 [24576, 4096], P('ctx', 'ch'), may hold values from -6 to 6
- proj_weight: bfloat16 [4096, 4096], P('ctx', 'ch'), may hold values from -0.09375 to 0.09375
- gate_q: bfloat16 [24576, 4096], P('ctx', 'ch'), may hold values from -6 to 6
- gate_k: bfloat16 [24576, 4096], P('ctx', 'ch'), may hold values from -6 to 6
- filter_spec: float32 [2, 128, 384, 4096], P(None, 'ctx', None, 'ch'), may hold values from -6 to 6
Outputs:
- gated: bfloat16 [24576, 4096], P('ctx', 'ch')
All inputs are finite; a program needn't handle non-finite values.
Results may differ from a plain program's by a relative error of at most 0.0049.
Values may be sent and summed in bfloat16 or wider, within the bound.
A program may use at most 64 MiB of HBM per device.

v0:
```python
import math

import jax
import jax.numpy as jnp
from jax import lax
from jax.sharding import PartitionSpec as P

TWO_PI = 2.0 * math.pi
HIGHEST = lax.Precision.HIGHEST


def split_up(x, dim, peers):
    before, after = (x.shape[:dim], x.shape[dim + 1 :])
    return jnp.moveaxis(x.reshape(*before, peers, -1, *after), dim, 0)


def piece_ends(length, count):
    turn = length // count
    if turn >= 8:
        turn -= turn % 8
    return [turn * k for k in range(1, count)]


def in_order(pieces, dim):
    pieces = jnp.moveaxis(pieces, 0, dim)
    shape = pieces.shape
    return pieces.reshape(*shape[:dim], shape[dim] * shape[dim + 1], *shape[dim + 2 :])


def several_exchanges(x, axis, pieces, split_dim, concat_dim):
    blocks = split_up(x, split_dim, lax.axis_size(axis))
    split_at = max(range(1, max(2, blocks.ndim - 1)), key=lambda d: blocks.shape[d])
    outs = []
    for section in jnp.split(blocks, piece_ends(blocks.shape[split_at], pieces), axis=split_at):
        if section.size:
            outs.append(lax.all_to_all(section, axis, split_axis=0, concat_axis=0, tiled=True))
    return in_order(jnp.concatenate(outs, axis=split_at), concat_dim)


def phase_table(left_index, right_index, modulus):
    angles = (left_index * right_index % modulus).astype(jnp.float32) * (TWO_PI / modulus)
    return (jnp.cos(angles), jnp.sin(angles))


def forward_channels(signal, freq_index, slab_count):
    slab_index = jnp.arange(slab_count, dtype=jnp.int32)
    cosine, sine_part = phase_table(freq_index[:, None], slab_index[None, :], 2 * slab_count)
    real_part = jnp.einsum("ks,cst->ckt", cosine, signal, precision=HIGHEST)
    imag_part = -jnp.einsum("ks,cst->ckt", sine_part, signal, precision=HIGHEST)
    return (real_part, imag_part)


def inverse_channels(real_part, imag_part, freq_index, slab_count):
    slab_index = jnp.arange(slab_count, dtype=jnp.int32)
    cosine, sine_part = phase_table(freq_index[:, None], slab_index[None, :], 2 * slab_count)
    return jnp.einsum("ks,ckt->cst", cosine, real_part, precision=HIGHEST) - jnp.einsum(
        "ks,ckt->cst", sine_part, imag_part, precision=HIGHEST
    )


def rotate_channels(real_part, imag_part, freq_index, time_index, modulus, direction):
    cosine, sine_part = phase_table(freq_index[:, None], time_index[None, :], modulus)
    cosine = cosine[None]
    sine_part = direction * sine_part[None]
    return (real_part * cosine - imag_part * sine_part, imag_part * cosine + real_part * sine_part)


def rows_channels(real_part, imag_part, direction):
    row_count = real_part.shape[2]
    row_index = jnp.arange(row_count, dtype=jnp.int32)
    cosine, sine_part = phase_table(row_index[:, None], row_index[None, :], row_count)
    sine_part = direction * sine_part

    def contract(matrix, operand):
        return jnp.einsum("jt,ckt->ckj", matrix, operand, precision=HIGHEST)

    new_real = contract(cosine, real_part) - contract(sine_part, imag_part)
    new_imag = contract(cosine, imag_part) + contract(sine_part, real_part)
    return (new_real, new_imag)


def filter_product(real_part, imag_part, spectra):
    return (
        spectra[0] * real_part - spectra[1] * imag_part,
        spectra[0] * imag_part + spectra[1] * real_part,
    )


def per_device(features, proj_weight, gate_q, gate_k, filter_spec):
    gathered = lax.all_gather(features, "ch", axis=1, tiled=True)
    tok_rows = gathered.shape[0]
    projected = jnp.dot(
        gathered,
        lax.all_gather(proj_weight, "ctx", axis=0, tiled=True),
        preferred_element_type=jnp.float32,
    )
    signal = (gate_k.astype(jnp.float32) * projected).astype(jnp.bfloat16)
    slab_count = lax.axis_size("ctx")
    freq_count = 2 * slab_count
    fft_length = freq_count * tok_rows
    freq_all = jnp.arange(freq_count, dtype=jnp.int32)
    time_all = jnp.arange(tok_rows, dtype=jnp.int32)
    chan_signal = lax.all_to_all(
        jnp.transpose(signal), "ctx", split_axis=0, concat_axis=1, tiled=True
    )
    spec_local = jnp.transpose(filter_spec, (0, 3, 1, 2))
    spectra = several_exchanges(spec_local, "ctx", 2, 1, 2)
    local_count = chan_signal.shape[0]
    local_signal = chan_signal.astype(jnp.float32).reshape(local_count, slab_count, tok_rows)
    real_part, imag_part = forward_channels(local_signal, freq_all, slab_count)
    real_part, imag_part = rotate_channels(
        real_part, imag_part, freq_all, time_all, fft_length, -1.0
    )
    real_part, imag_part = rows_channels(real_part, imag_part, -1.0)
    real_part, imag_part = filter_product(real_part, imag_part, spectra)
    real_part, imag_part = rows_channels(real_part, imag_part, 1.0)
    real_part, imag_part = rotate_channels(
        real_part, imag_part, freq_all, time_all, fft_length, 1.0
    )
    slab_values = inverse_channels(real_part, imag_part, freq_all, slab_count) / fft_length
    slab_values = slab_values.reshape(local_count, slab_count * tok_rows)
    returned = lax.all_to_all(slab_values, "ctx", split_axis=1, concat_axis=0, tiled=True)
    convolved = jnp.transpose(returned)
    return (gate_q.astype(jnp.float32) * convolved).astype(jnp.bfloat16)


def solution(mesh):
    in_specs = (
        P("ctx", "ch"),
        P("ctx", "ch"),
        P("ctx", "ch"),
        P("ctx", "ch"),
        P(None, "ctx", None, "ch"),
    )
    out_specs = P("ctx", "ch")
    return jax.shard_map(
        per_device, mesh=mesh, in_specs=in_specs, out_specs=out_specs, check_vma=False
    )
```

profile of v0, /device:TPU:20, one launch (start us, length us, event | category | flops | bytes accessed | tf_op | source)
XLA Modules:
  0.0 288.5 jit_solution(2001028204765182182)
XLA Ops:
  6.5 0.7 all-gather.3.cloned.1.call-update
  7.3 0.7 all-gather.5.cloned.1.call-update
  8.0 2.4 copy.37
  10.4 1.7 fusion.155
  12.1 1.4 copy.39
  13.5 16.6 %all-to-all-start.1 = ((f32[64,2,4,2,384]{4,2,3,1,0:T(4,128)}), f32[64,2,4,2,384]{4,2,3,1,0:T(4,128)S(1)}, u32[]{:S(2)}, u32[]{:S(2)}) async-start(f32[64,2,4,2,384]{4,2,3,1,0:T(4,128)} %copy.39), calls=%async_computation.1 | async-start | bytes 3145728 | tf_op jit(solution)/shard_map/all_to_all | solution.py:36
  30.2 1.5 copy.38
  31.7 39.6 %all-to-all-done.1 = f32[64,2,4,2,384]{4,2,3,1,0:T(4,128)S(1)} async-done(((f32[64,2,4,2,384]{4,2,3,1,0:T(4,128)}), f32[64,2,4,2,384]{4,2,3,1,0:T(4,128)S(1)}, u32[]{:S(2)}, u32[]{:S(2)}) %all-to-all-start.1) | async-done | bytes 1572896 | tf_op jit(solution)/shard_map/all_to_all | solution.py:36
  71.3 8.2 %all-to-all-start = ((f32[64,2,4,2,384]{4,2,3,1,0:T(4,128)}), f32[64,2,4,2,384]{4,2,3,1,0:T(4,128)S(1)}, u32[]{:S(2)}, u32[]{:S(2)}) async-start(f32[64,2,4,2,384]{4,2,3,1,0:T(4,128)} %copy.38), calls=%async_computation | async-start | bytes 3145728 | tf_op jit(solution)/shard_map/all_to_all | solution.py:36
  79.5 85.1 %all-gather.5.cloned.1.call-done = bf16[4096,512]{1,0:T(8,128)(2,1)} async-done(((bf16[64,512]{1,0:T(8,128)(2,1)}), bf16[4096,512]{1,0:T(8,128)(2,1)}) %all-gather.5.cloned.1.call-update) | async-done | bytes 4194320 | tf_op jit(solution)/shard_map/all_gather | solution.py:94
  164.6 5.7 %fusion.20 = bf16[512,384]{0,1:T(8,128)(2,1)} fusion(bf16[384,4096]{1,0:T(8,128)(2,1)} %all-gather.3.cloned.1.call-done, bf16[4096,512]{1,0:T(8,128)(2,1)} %all-gather.5.cloned.1.call-done, bf16[384,512]{1,0:T(8,128)(2,1)} %param.8), kind=kOutput, calls=%fused_computation.27 | convolution fusion | flops 1611202560 | bytes 8126464 | tf_op jit(solution)/shard_map/dot_general | solution.py:92
  170.3 1.9 copy.41
  172.2 9.1 %all-to-all-start.2 = ((bf16[64,8,384]{2,1,0:T(8,128)(2,1)}), bf16[64,8,384]{2,1,0:T(8,128)(2,1)}, u32[]{:S(2)}, u32[]{:S(2)}) async-start(bf16[64,8,384]{2,1,0:T(8,128)(2,1)} %bitcast.93), calls=%async_computation.2 | async-start | bytes 786432 | tf_op jit(solution)/shard_map/all_to_all | solution.py:103
  181.3 1.4 fusion.93
  182.8 0.8 fusion.94
  184.5 10.5 %all-to-all-done.2 = bf16[64,8,384]{2,1,0:T(8,128)(2,1)} async-done(((bf16[64,8,384]{2,1,0:T(8,128)(2,1)}), bf16[64,8,384]{2,1,0:T(8,128)(2,1)}, u32[]{:S(2)}, u32[]{:S(2)}) %all-to-all-start.2) | async-done | bytes 393248 | tf_op jit(solution)/shard_map/all_to_all | solution.py:103
  194.9 2.0 convolution_negate_fusion
  196.9 2.0 fusion.55
  199.0 7.2 %fusion.36 = f32[8,128,384]{2,1,0:T(8,128)S(1)} fusion(f32[8,384,128]{2,1,0:T(8,128)S(1)} %convolution_negate_fusion, f32[8,384,128]{2,1,0:T(8,128)S(1)} %fusion.55, f32[128,384]{0,1:T(8,128)S(1)} %get-tuple-element.12, f32[128,384]{0,1:T(8,128)S(1)} %get-tuple-element.11), kind=kOutput, calls=%fused_computation.45 | convolution fusion | flops 1814446080 | bytes 5111808 | tf_op jit(solution)/shard_map/jt,ckt->ckj/dot_general | solution.py:75
  206.2 7.6 %fusion.38 = f32[8,128,384]{2,1,0:T(8,128)S(1)} fusion(f32[8,384,128]{2,1,0:T(8,128)S(1)} %convolution_negate_fusion, f32[8,384,128]{2,1,0:T(8,128)S(1)} %fusion.55, f32[128,384]{0,1:T(8,128)S(1)} %get-tuple-element.12, f32[128,384]{0,1:T(8,128)S(1)} %get-tuple-element.11), kind=kOutput, calls=%fused_computation.47 | convolution fusion | flops 1814446080 | bytes 5111808 | tf_op jit(solution)/shard_map/jt,ckt->ckj/dot_general | solution.py:75
  213.8 7.5 %convolution_add_fusion.1 = f32[8,128,384]{2,1,0:T(8,128)S(1)} fusion(f32[8,128,384]{2,1,0:T(8,128)S(1)} %fusion.36, f32[8,384,128]{2,1,0:T(8,128)S(1)} %convolution_negate_fusion, f32[8,384,128]{2,1,0:T(8,128)S(1)} %fusion.55, f32[128,384]{0,1:T(8,128)S(1)} %get-tuple-element.12, f32[128,384]{0,1:T(8,128)S(1)} %get-tuple-element.11), kind=kOutput, calls=%fused_computation.20 | convolution fusion | flops 1814986752 | bytes 6684672 | tf_op jit(solution)/shard_map/jt,ckt->ckj/dot_general | solution.py:75
  221.3 8.0 %multiply_add_fusion = (f32[8,128,384]{2,1,0:T(8,128)S(1)}, f32[8,128,384]{2,1,0:T(8,128)S(1)}) fusion(f32[8,128,384]{2,1,0:T(8,128)S(1)} %convolution_add_fusion.1, f32[8,128,384]{2,0,1:T(8,128)S(1)} %bitcast.92, f32[8,128,384]{2,0,1:T(8,128)S(1)} %bitcast.91, f32[8,128,384]{2,1,0:T(8,128)S(1)} %fusion.38, f32[8,384,128]{2,1,0:T(8,128)S(1)} %convolution_negate_fusion, ...), kind=kOutput, calls=%fused_computation.15 | convolution fusion | flops 1817346048 | bytes 12976128 | tf_op jit(solution)/shard_map/jt,ckt->ckj/dot_general | solution.py:75
  229.3 5.1 %fusion.34 = f32[8,128,384]{1,2,0:T(8,128)S(1)} fusion(f32[8,128,384]{2,1,0:T(8,128)S(1)} %get-tuple-element.6), kind=kOutput, calls=%fused_computation.43 | convolution fusion | flops 1813266432 | bytes 3145728 | tf_op jit(solution)/shard_map/jt,ckt->ckj/dot_general | solution.py:75
  234.4 4.9 %fusion.32 = f32[8,128,384]{1,2,0:T(8,128)S(1)} fusion(f32[8,128,384]{2,1,0:T(8,128)S(1)} %get-tuple-element.5), kind=kOutput, calls=%fused_computation.41 | convolution fusion | flops 1813266432 | bytes 3145728 | tf_op jit(solution)/shard_map/jt,ckt->ckj/dot_general | solution.py:75
  239.3 5.2 %convolution_subtract_fusion = f32[8,128,384]{1,2,0:T(8,128)S(1)} fusion(f32[8,128,384]{1,2,0:T(8,128)S(1)} %fusion.34, f32[8,128,384]{2,1,0:T(8,128)S(1)} %get-tuple-element.5), kind=kOutput, calls=%fused_computation.19 | convolution fusion | flops 1813659648 | bytes 4718592 | tf_op jit(solution)/shard_map/jt,ckt->ckj/dot_general | solution.py:75
  244.6 4.9 %convolution_add_fusion = f32[8,128,384]{1,2,0:T(8,128)S(1)} fusion(f32[8,128,384]{1,2,0:T(8,128)S(1)} %fusion.32, f32[8,128,384]{2,1,0:T(8,128)S(1)} %get-tuple-element.6), kind=kOutput, calls=%fused_computation.18 | convolution fusion | flops 1813659648 | bytes 4718592 | tf_op jit(solution)/shard_map/jt,ckt->ckj/dot_general | solution.py:75
  249.5 2.2 fusion.2
  251.7 2.2 fusion.16
  253.9 1.3 copy.54
  255.3 5.2 %all-to-all-start.3 = ((f32[8,64,384]{2,0,1:T(8,128)}), f32[8,64,384]{2,0,1:T(8,128)S(1)}, u32[]{:S(2)}, u32[]{:S(2)}) async-start(f32[8,64,384]{2,0,1:T(8,128)} %copy.54), calls=%async_computation.3 | async-start | bytes 1572864 | tf_op jit(solution)/shard_map/all_to_all | solution.py:122
  260.7 19.6 %all-to-all-done.3 = f32[8,64,384]{2,0,1:T(8,128)S(1)} async-done(((f32[8,64,384]{2,0,1:T(8,128)}), f32[8,64,384]{2,0,1:T(8,128)S(1)}, u32[]{:S(2)}, u32[]{:S(2)}) %all-to-all-start.3) | async-done | bytes 786464 | tf_op jit(solution)/shard_map/all_to_all | solution.py:122
  280.3 0.9 copy.55
  (14 shorter events, 1.2 us)
Async XLA Ops:
  6.5 73.0 %all-gather.3.cloned.1.call-start = ((), (), s32[]{:S(2)}) async-start(), calls=%async_computation.4 | async-start | bytes 3538944 | tf_op jit(solution)/shard_map/all_gather | solution.py:90
  7.3 157.4 %all-gather.5.cloned.1.call-start = ((), (), s32[]{:S(2)}) async-start(), calls=%async_computation.5 | async-start | bytes 4259840 | tf_op jit(solution)/shard_map/all_gather | solution.py:94
  13.5 16.6 %copy-start = (f32[64,2,4,2,384]{4,2,0,3,1:T(4,128)S(1)}, f32[64,2,4,2,384]{4,2,0,3,1:T(4,128)}, u32[]{:S(2)}) copy-start(f32[64,2,4,2,384]{4,2,0,3,1:T(4,128)} %get-tuple-element.9) | copy-start | bytes 4718596
  13.5 57.7 %all-to-all-start.1 = ((f32[64,2,4,2,384]{4,2,3,1,0:T(4,128)}), f32[64,2,4,2,384]{4,2,3,1,0:T(4,128)S(1)}, u32[]{:S(2)}, u32[]{:S(2)}) async-start(f32[64,2,4,2,384]{4,2,3,1,0:T(4,128)} %copy.39), calls=%async_computation.1 | async-start | bytes 3145728 | tf_op jit(solution)/shard_map/all_to_all | solution.py:36
  71.3 101.0 %all-to-all-start = ((f32[64,2,4,2,384]{4,2,3,1,0:T(4,128)}), f32[64,2,4,2,384]{4,2,3,1,0:T(4,128)S(1)}, u32[]{:S(2)}, u32[]{:S(2)}) async-start(f32[64,2,4,2,384]{4,2,3,1,0:T(4,128)} %copy.38), calls=%async_computation | async-start | bytes 3145728 | tf_op jit(solution)/shard_map/all_to_all | solution.py:36
  172.2 22.7 %all-to-all-start.2 = ((bf16[64,8,384]{2,1,0:T(8,128)(2,1)}), bf16[64,8,384]{2,1,0:T(8,128)(2,1)}, u32[]{:S(2)}, u32[]{:S(2)}) async-start(bf16[64,8,384]{2,1,0:T(8,128)(2,1)} %bitcast.93), calls=%async_computation.2 | async-start | bytes 786432 | tf_op jit(solution)/shard_map/all_to_all | solution.py:103
  244.6 5.0 %copy-start.1 = (f32[128,384]{0,1:T(8,128)S(1)}, f32[128,384]{0,1:T(8,128)}, u32[]{:S(2)}) copy-start(f32[128,384]{0,1:T(8,128)} %fusion.93) | copy-start | bytes 589828
  253.9 6.5 %copy-start.2 = (bf16[384,512]{1,0:T(8,128)(2,1)S(1)}, bf16[384,512]{1,0:T(8,128)(2,1)}, u32[]{:S(2)}) copy-start(bf16[384,512]{1,0:T(8,128)(2,1)} %param.7) | copy-start | bytes 1179652
  255.3 25.0 %all-to-all-start.3 = ((f32[8,64,384]{2,0,1:T(8,128)}), f32[8,64,384]{2,0,1:T(8,128)S(1)}, u32[]{:S(2)}, u32[]{:S(2)}) async-start(f32[8,64,384]{2,0,1:T(8,128)} %copy.54), calls=%async_computation.3 | async-start | bytes 1572864 | tf_op jit(solution)/shard_map/all_to_all | solution.py:122
Sparse Core Ops, SparseCore 0:
  9.5 36.0 all-gather.2
  48.6 115.9 all-gather.4
where the time goes:
time: 294 us; the launch traced here: 289 us
  waiting for transfers between devices  156 us (53%)
  matrix products  64.6 us (22%)
  starting transfers between devices  39.1 us (13%)
  between operations  14 us (5%)
  local copies, waits for them, and re-layouts  11.7 us (4%)
  other arithmetic  2.97 us (1%)
    all_gather x1, waiting for transfers between devices, per_device(): lax.all_gather(proj_weight, 'ctx', axis=0, tiled=True)  85.1 us
    dot_general x8, matrix products, contract(): return jnp.einsum('jt,ckt->ckj', matrix, operand, precision=HIGHEST)  50.5 us
    all_to_all x2, waiting for transfers between devices, several_exchanges(): lax.all_to_all(section, axis, split_axis=0, concat_axis=0, tiled=True)  39.6 us
    all_to_all x2, starting transfers between devices, several_exchanges(): lax.all_to_all(section, axis, split_axis=0, concat_axis=0, tiled=True)  24.8 us
    all_to_all x1, waiting for transfers between devices, per_device(): lax.all_to_all(slab_values, 'ctx', split_axis=1, concat_axis=0, tiled=True)  19.6 us
    all_to_all x1, waiting for transfers between devices, per_device(): lax.all_to_all(jnp.transpose(signal), 'ctx', split_axis=0, concat_axis=1,...  10.5 us
    all_to_all x1, starting transfers between devices, per_device(): lax.all_to_all(jnp.transpose(signal), 'ctx', split_axis=0, concat_axis=1,...  9.07 us
  transfers between devices with their start and end apart: 6, of which 4 were waited for; matrix products, arithmetic and copies ran while one was open for 6% of the time, Pallas kernels for 0%

commit v1 on v0

v1 whole, which is shorter than its diff:
```python
import functools

import jax
import jax.numpy as jnp
import numpy as np
from jax import lax
from jax.experimental import pallas as pl
from jax.experimental.pallas import tpu as pltpu
from jax.sharding import PartitionSpec as P

BF16 = jnp.bfloat16
F32 = jnp.float32
MESH = pl.DeviceIdType.MESH
OWN = 8


def hi_lo(table):
    hi = table.astype(BF16)
    lo = (table - hi.astype(np.float64)).astype(BF16)
    return hi, lo


def tables(slabs, tok):
    rows = 2 * slabs
    k1 = np.concatenate([np.arange(0, rows, 2), np.arange(1, rows, 2)])
    ang = 2.0 * np.pi * ((k1[:, None] * np.arange(slabs)[None, :]) % rows) / rows
    fwd = np.concatenate([np.cos(ang), -np.sin(ang)], axis=0)
    inv = np.concatenate([np.cos(ang), -np.sin(ang)], axis=0).T
    first = np.concatenate(hi_lo(fwd), axis=1)
    last = np.concatenate(hi_lo(inv), axis=1)
    ang = 2.0 * np.pi * (k1[:, None] * np.arange(tok)[None, :]) / (rows * tok)
    turn = np.stack([np.cos(ang), np.sin(ang)]).astype(np.float32)
    ang = 2.0 * np.pi * ((np.arange(tok)[:, None] * np.arange(tok)[None, :]) % tok) / tok
    cos_hi, cos_lo = hi_lo(np.cos(ang))
    sin_hi, sin_lo = hi_lo(np.sin(ang))
    basis = np.stack([cos_hi, sin_hi, cos_lo, sin_lo])
    return first, last, turn, basis


def every(ref, start, count, stride):
    return jnp.concatenate(
        [ref[j, pl.ds(start, count, stride=stride), :] for j in range(ref.shape[0])], axis=1
    )


def dot(a, b):
    return jnp.dot(a, b, preferred_element_type=F32)


def kernel(
    ring, rows_x, tok, group,
    feat_in, wt_in, gq_in, gk_in, spec_in, first_in, last_in, turn_in, basis_in,
    out_ref,
    feat, wt, gq, gk, spec, first, last, turn, basis,
    spec_out, spec_got, sig_out, sig_got, ret_out, ret_got,
    acc, sig_rows, spec_rows, forward, mat, conv_rows,
    load_sem, feat_send, feat_recv, wt_send, wt_recv,
    spec_send, spec_recv, sig_send, sig_recv, ret_send, ret_recv, self_sem,
):
    slabs = ring * ring
    chans = acc.shape[1]
    half = chans // 2
    me = lax.axis_index("ctx")
    lane = lax.axis_index("ch")
    core = lax.rem(lane, 2)
    xpos = lane // 2
    ypos = me // ring
    zpos = lax.rem(me, ring)
    step_a = 1 - 2 * core
    length = 2 * slabs * tok

    def around(pos, move, size):
        return lax.rem(pos + move + size, size)

    def spot(color, p, q):
        return q * ring + p if color == 0 else p * ring + q

    loads = [
        (wt_in.at[:, pl.ds(0, half)], wt.at[0, me]),
        (wt_in.at[:, pl.ds(half, half)], wt.at[1, me]),
        (feat_in, feat.at[lane]),
        (spec_in, spec),
        (gk_in, gk),
        (gq_in, gq),
        (first_in, first),
        (last_in, last),
        (turn_in, turn),
        (basis_in, basis),
    ]
    copies = [pltpu.make_async_copy(s, d, load_sem.at[i]) for i, (s, d) in enumerate(loads)]
    for c in copies:
        c.start()

    barrier = pltpu.get_barrier_semaphore()

    def greet(k, _):
        peer = lax.rem(me + k, slabs)
        pl.semaphore_signal(barrier, inc=1, device_id=(peer, lane), device_id_type=MESH)
        return 0

    lax.fori_loop(1, slabs, greet, 0)
    partner = 2 * xpos + 1 - core
    pl.semaphore_signal(barrier, inc=1, device_id=(me, partner), device_id_type=MESH)
    greeted = slabs
    if rows_x > 1:
        for move in (1, -1):
            peer = 2 * around(xpos, move, rows_x) + core
            pl.semaphore_signal(barrier, inc=1, device_id=(me, peer), device_id_type=MESH)
        greeted += 2

    copies[3].wait()
    per = 128 // OWN
    for part in range(2):
        for odd in range(2):
            for j in range(chans // 128):
                block = spec[part, odd, :, pl.ds(128 * j, 128)].T
                spec_out[pl.ds(per * j, per), pl.ds(OWN * odd, OWN), pl.ds(tok * part, tok)] = (
                    block.reshape(per, OWN, tok).astype(BF16)
                )
    for i in (0, 1, 2):
        copies[i].wait()
    pl.semaphore_wait(barrier, greeted)

    def send_feat(slot, device):
        pltpu.make_async_remote_copy(
            src_ref=feat.at[slot], dst_ref=feat.at[slot], send_sem=feat_send,
            recv_sem=feat_recv.at[slot], device_id=(me, device), device_id_type=MESH,
        ).start()

    def wait_feat(slot):
        pltpu.make_async_copy(feat.at[slot], feat.at[slot], feat_recv.at[slot]).wait()

    def send_wt(color, slot, device):
        pltpu.make_async_remote_copy(
            src_ref=wt.at[color, slot], dst_ref=wt.at[color, slot], send_sem=wt_send,
            recv_sem=wt_recv.at[color, slot], device_id=(device, lane), device_id_type=MESH,
        ).start()

    def wait_wt(color, slot):
        pltpu.make_async_copy(wt.at[color, slot], wt.at[color, slot], wt_recv.at[color, slot]).wait()

    reach = ((step_a, ring // 2), (-step_a, ring // 2 - 1))
    place = ((zpos, ypos), (ypos, zpos))

    def along_p(color, slot, move):
        p, q = place[color]
        send_wt(color, slot, spot(color, around(p, move, ring), q))

    def along_q(color, slot, move):
        p, q = place[color]
        send_wt(color, slot, spot(color, p, around(q, move, ring)))

    for color in range(2):
        for move, far in reach:
            if far >= 1:
                along_p(color, me, move)
    for color in range(2):
        for move, far in reach:
            if far >= 1:
                along_q(color, me, move)
    reach_x = ((step_a, rows_x // 2), (-step_a, rows_x // 2 - 1))
    for move, far in reach_x:
        if far >= 1:
            send_feat(lane, 2 * around(xpos, move, rows_x) + core)
    send_feat(lane, partner)

    for k in range(1, ring // 2 + 1):
        for color in range(2):
            p, q = place[color]
            for move, far in reach:
                if k <= far:
                    slot = spot(color, around(p, -move * k, ring), q)
                    wait_wt(color, slot)
                    if k < far:
                        along_p(color, slot, move)
                    for move_q, far_q in reach:
                        if far_q >= 1:
                            along_q(color, slot, move_q)

    def pass_on(k):
        def body(j, _):
            m = (j + 1) // 2
            flip = 1 - 2 * lax.rem(j, 2)
            for color in range(2):
                p, q = place[color]
                from_p = around(p, flip * step_a * m, ring)
                for move, far in reach:
                    if k <= far:
                        slot = spot(color, from_p, around(q, -move * k, ring))
                        wait_wt(color, slot)
                        if k < far:
                            along_q(color, slot, move)
            return 0

        lax.fori_loop(0, ring, body, 0)

    for k in range(1, ring // 2 + 1):
        pass_on(k)
        for move, far in reach_x:
            if k <= far:
                slot = 2 * around(xpos, -move * k, rows_x) + core
                wait_feat(slot)
                if k < far:
                    send_feat(slot, 2 * around(xpos, move, rows_x) + core)
                send_feat(slot, partner)

    def scatter(buffer, got, send_sem, recv_sem, low, high):
        def body(k, _):
            away = lax.rem(k * 29, slabs)
            y_to = lax.rem(ypos + away // ring, ring)
            z_to = lax.rem(zpos + lax.rem(away, ring), ring)
            peer = y_to * ring + z_to
            pltpu.make_async_remote_copy(
                src_ref=buffer.at[peer], dst_ref=got.at[me], send_sem=send_sem,
                recv_sem=recv_sem.at[me], device_id=(peer, lane), device_id_type=MESH,
            ).start()
            return 0

        lax.fori_loop(low, high, body, 0)

    def collect(got, recv_sem):
        def body(k, _):
            slot = lax.rem(me + k, slabs)
            pltpu.make_async_copy(got.at[slot], got.at[slot], recv_sem.at[slot]).wait()
            return 0

        lax.fori_loop(1, slabs, body, 0)

    early = slabs // 4
    scatter(spec_out, spec_got, spec_send, spec_recv, 1, early)
    own_spec = pltpu.make_async_copy(spec_out.at[me], spec_got.at[me], self_sem.at[0])
    own_spec.start()

    for x in range(rows_x):
        wait_feat(2 * x + 1 - core)

    copies[4].wait()
    acc[...] = jnp.zeros_like(acc)
    per_feat = feat.shape[2] // wt.shape[2]

    def project(f, _):
        for color in range(2):
            block = wt[color, pl.ds(f * per_feat, per_feat)].reshape(feat.shape[2], half)
            acc[:, pl.ds(color * half, half)] += dot(feat[f], block)
        return 0

    lax.fori_loop(0, 2 * rows_x, project, 0)
    for j in range(chans // 128):
        cols = pl.ds(128 * j, 128)
        value = gk[:, cols].astype(F32) * acc[:, cols]
        sig_out[pl.ds(per * j, per)] = value.T.reshape(per, OWN, tok).astype(BF16)
    scatter(sig_out, sig_got, sig_send, sig_recv, 1, slabs)
    own_sig = pltpu.make_async_copy(sig_out.at[me], sig_got.at[me], self_sem.at[1])
    own_sig.start()
    scatter(spec_out, spec_got, spec_send, spec_recv, early, slabs)

    for i in (6, 7, 8, 9):
        copies[i].wait()
    for level in range(2):
        cosine = basis[2 * level]
        sine = basis[2 * level + 1]
        mat[level, pl.ds(0, tok), pl.ds(0, tok)] = cosine
        mat[level, pl.ds(0, tok), pl.ds(tok, tok)] = -sine
        mat[level, pl.ds(tok, tok), pl.ds(0, tok)] = sine
        mat[level, pl.ds(tok, tok), pl.ds(tok, tok)] = cosine

    own_sig.wait()
    collect(sig_got, sig_recv)
    for j in range(tok // 128):
        sig_rows[j] = sig_got[:, :, pl.ds(128 * j, 128)].astype(F32).reshape(slabs * OWN, 128)
    cos_t = turn[0]
    sin_t = turn[1]
    freqs = 2 * slabs

    def go_forward(g, _):
        pieces = []
        for u in range(group):
            x = every(sig_rows, g * group + u, slabs, OWN).astype(BF16)
            a = dot(first[...], jnp.concatenate([x, x], axis=0))
            re, im = a[:freqs], a[freqs:]
            pieces.append(
                jnp.concatenate([re * cos_t + im * sin_t, im * cos_t - re * sin_t], axis=1)
            )
        b = jnp.concatenate(pieces, axis=0)
        b_hi = b.astype(BF16)
        b_lo = (b - b_hi.astype(F32)).astype(BF16)
        full = dot(b_hi, mat[0]) + dot(b_hi, mat[1]) + dot(b_lo, mat[0])
        forward[pl.ds(g * group, group)] = full.reshape(group, freqs, 2 * tok)
        return 0

    lax.fori_loop(0, OWN // group, go_forward, 0)

    own_spec.wait()
    collect(spec_got, spec_recv)
    for j in range(2 * tok // 128):
        spec_rows[j] = (
            spec_got[:, :, pl.ds(128 * j, 128)].astype(F32).reshape(slabs * 2 * OWN, 128)
        )

    def go_back(g, _):
        pieces = []
        for u in range(group):
            c = g * group + u
            h = jnp.concatenate(
                [every(spec_rows, odd * OWN + c, slabs, 2 * OWN) for odd in range(2)],
                axis=0,
            )
            x = forward[c]
            hr, hi = h[:, :tok], h[:, tok:]
            xr, xi = x[:, :tok], x[:, tok:]
            pieces.append(
                jnp.concatenate([hr * xr - hi * xi, -(hr * xi + hi * xr)], axis=1).astype(BF16)
            )
        v = jnp.concatenate(pieces, axis=0)
        z = dot(v, mat[0]) + dot(v, mat[1])
        for u in range(group):
            zr = z[u * freqs : (u + 1) * freqs, :tok]
            zi = z[u * freqs : (u + 1) * freqs, tok:]
            both = jnp.concatenate(
                [zr * cos_t + zi * sin_t, zr * sin_t - zi * cos_t], axis=0
            ).astype(BF16)
            y = dot(last[...], jnp.concatenate([both, both], axis=0))
            y = y * (1.0 / length)
            for j in range(tok // 128):
                conv_rows[j, pl.ds(g * group + u, slabs, stride=OWN), :] = y[:, 128 * j : 128 * j + 128]
        return 0

    lax.fori_loop(0, OWN // group, go_back, 0)

    for j in range(tok // 128):
        ret_out[:, :, pl.ds(128 * j, 128)] = conv_rows[j].reshape(slabs, OWN, 128).astype(BF16)
    scatter(ret_out, ret_got, ret_send, ret_recv, 1, slabs)
    own_ret = pltpu.make_async_copy(ret_out.at[me], ret_got.at[me], self_sem.at[2])
    own_ret.start()
    copies[5].wait()
    pltpu.make_async_copy(
        wt.at[:, pl.ds(0, slabs - 1)], wt.at[:, pl.ds(0, slabs - 1)], wt_send
    ).wait()
    sent = 2 * rows_x - 1
    pltpu.make_async_copy(feat.at[pl.ds(0, sent)], feat.at[pl.ds(0, sent)], feat_send).wait()
    rest = pl.ds(0, slabs - 1)
    pltpu.make_async_copy(spec_out.at[rest], spec_out.at[rest], spec_send).wait()
    pltpu.make_async_copy(sig_out.at[rest], sig_out.at[rest], sig_send).wait()
    own_ret.wait()
    collect(ret_got, ret_recv)
    for j in range(chans // 128):
        cols = pl.ds(128 * j, 128)
        value = ret_got[pl.ds(per * j, per)].astype(F32).reshape(128, tok).T
        out_ref[:, cols] = (gq[:, cols].astype(F32) * value).astype(BF16)
    pltpu.make_async_copy(ret_out.at[rest], ret_out.at[rest], ret_send).wait()


def per_device(ring, rows_x, features, proj_weight, gate_q, gate_k, filter_spec):
    tok, feats = features.shape
    w_rows, chans = proj_weight.shape
    slabs = ring * ring
    first, last, turn, basis = tables(slabs, tok)
    any_space = pl.BlockSpec(memory_space=pl.ANY)
    freqs = 2 * slabs
    lanes = 2 * rows_x
    vm = pltpu.VMEM
    dma = pltpu.SemaphoreType.DMA
    scratch = [
        vm((lanes, tok, feats), BF16),
        vm((2, slabs, w_rows, chans // 2), BF16),
        vm((tok, chans), BF16),
        vm((tok, chans), BF16),
        vm((2, 2, tok, chans), F32),
        vm(first.shape, BF16),
        vm(last.shape, BF16),
        vm(turn.shape, F32),
        vm(basis.shape, BF16),
        vm((slabs, 2 * OWN, 2 * tok), BF16),
        vm((slabs, 2 * OWN, 2 * tok), BF16),
        vm((slabs, OWN, tok), BF16),
        vm((slabs, OWN, tok), BF16),
        vm((slabs, OWN, tok), BF16),
        vm((slabs, OWN, tok), BF16),
        vm((tok, chans), F32),
        vm((tok // 128, slabs * OWN, 128), F32),
        vm((2 * tok // 128, slabs * 2 * OWN, 128), F32),
        vm((OWN, freqs, 2 * tok), F32),
        vm((2, 2 * tok, 2 * tok), BF16),
        vm((tok // 128, slabs * OWN, 128), F32),
        dma((10,)),
        dma,
        dma((lanes,)),
        dma,
        dma((2, slabs)),
        dma,
        dma((slabs,)),
        dma,
        dma((slabs,)),
        dma,
        dma((slabs,)),
        dma((3,)),
    ]
    return pl.pallas_call(
        functools.partial(kernel, ring, rows_x, tok, 4),
        out_shape=jax.ShapeDtypeStruct((tok, chans), BF16),
        in_specs=[any_space] * 9,
        out_specs=pl.BlockSpec(memory_space=pltpu.VMEM),
        scratch_shapes=scratch,
        compiler_params=pltpu.CompilerParams(
            collective_id=0, has_side_effects=True, vmem_limit_bytes=60 * 1024 * 1024
        ),
        name="hyena",
    )(
        features, proj_weight, gate_q, gate_k, filter_spec,
        jnp.asarray(first), jnp.asarray(last), jnp.asarray(turn), jnp.asarray(basis),
    )


def solution(mesh):
    ring = int(round(mesh.shape["ctx"] ** 0.5))
    rows_x = mesh.shape["ch"] // 2
    in_specs = (
        P("ctx", "ch"),
        P("ctx", "ch"),
        P("ctx", "ch"),
        P("ctx", "ch"),
        P(None, "ctx", None, "ch"),
    )
    return jax.shard_map(
        functools.partial(per_device, ring, rows_x),
        mesh=mesh, in_specs=in_specs, out_specs=P("ctx", "ch"), check_vma=False,
    )
```

time: 294 us -> 127 us (0.43)
  the two profiles are of different devices: /device:TPU:20 before, /device:TPU:16 now
where the time goes in v1:
time: 127 us
  Pallas kernels  125 us (98%)
  local copies, waits for them, and re-layouts  1.77 us (1%)
    pallas_call x1, Pallas kernels, per_device(): pl.pallas_call(functools.partial(kernel, ring, rows_x, tok, 4), out_shape...  125 us

profile of v1, /device:TPU:16, one launch (start us, length us, event | category | flops | bytes accessed | tf_op | source)
XLA Modules:
  0.0 126.7 jit_solution(4639130210519473233)
XLA Ops:
  0.0 124.9 %hyena.1 = bf16[384,512]{1,0:T(8,128)(2,1)} custom-call(bf16[384,512]{1,0:T(8,128)(2,1)} %feat_in.1, bf16[64,512]{1,0:T(8,128)(2,1)} %wt_in.1, bf16[384,512]{1,0:T(8,128)(2,1)} %gq_in.1, bf16[384,512]{1,0:T(8,128)(2,1)} %gk_in.1, f32[2,2,384,512]{3,2,1,0:T(8,128)} %spec_in.1, bf16[256,128]{1,0:T(8,128)(2,1)} %constant.8.clone.first_in, ...), custom_call_target="tpu_custom_call" | custom-call | tf_op jit(solution)/shard_map/hyena/pallas_call | solution.py:398
  124.9 1.8 %copy.11 = bf16[384,512]{1,0:T(8,128)(2,1)} copy(bf16[384,512]{1,0:T(8,128)(2,1)} %hyena.1) | data formatting | bytes 786432

commit v2 on v1

--- a/solution.py
+++ b/solution.py
@@ -12,6 +12,8 @@
 F32 = jnp.float32
 MESH = pl.DeviceIdType.MESH
 OWN = 8
+HALF = OWN // 2
+PACE = (2, 2, 2, 2, 2, 8)
 
 
 def hi_lo(table):
@@ -48,7 +50,7 @@
 
 
 def kernel(
-    ring, rows_x, tok, group,
+    ring, rows_x, tok, pace,
     feat_in, wt_in, gq_in, gk_in, spec_in, first_in, last_in, turn_in, basis_in,
     out_ref,
     feat, wt, gq, gk, spec, first, last, turn, basis,
@@ -111,15 +113,59 @@
     copies[3].wait()
     per = 128 // OWN
     for part in range(2):
-        for odd in range(2):
-            for j in range(chans // 128):
-                block = spec[part, odd, :, pl.ds(128 * j, 128)].T
-                spec_out[pl.ds(per * j, per), pl.ds(OWN * odd, OWN), pl.ds(tok * part, tok)] = (
-                    block.reshape(per, OWN, tok).astype(BF16)
-                )
+        for j in range(chans // 128):
+            even, odd = (
+                spec[part, b, :, pl.ds(128 * j, 128)].T.reshape(per, OWN, tok) for b in range(2)
+            )
+            for g in range(2):
+                rows = slice(HALF * g, HALF * g + HALF)
+                spec_out[g, pl.ds(per * j, per), pl.ds(OWN * part, OWN), :] = jnp.concatenate(
+                    [even[:, rows], odd[:, rows]], axis=1
+                ).astype(BF16)
     for i in (0, 1, 2):
         copies[i].wait()
     pl.semaphore_wait(barrier, greeted)
+
+    def send_to(k, buffer, got, send_sem, recv_sem):
+        away = lax.rem(k * 29, slabs)
+        y_to = lax.rem(ypos + away // ring, ring)
+        z_to = lax.rem(zpos + lax.rem(away, ring), ring)
+        peer = y_to * ring + z_to
+        pltpu.make_async_remote_copy(
+            src_ref=buffer.at[peer], dst_ref=got.at[me], send_sem=send_sem,
+            recv_sem=recv_sem.at[me], device_id=(peer, lane), device_id_type=MESH,
+        ).start()
+
+    def scatter(buffer, got, send_sem, recv_sem):
+        def body(k, _):
+            send_to(k, buffer, got, send_sem, recv_sem)
+            return 0
+
+        lax.fori_loop(1, slabs, body, 0)
+
+    def send_spec(first_one, count):
+        def body(n, _):
+            item = first_one + n
+            g = item // (slabs - 1)
+            send_to(
+                1 + lax.rem(item, slabs - 1), spec_out.at[g], spec_got.at[g],
+                spec_send.at[g], spec_recv.at[g],
+            )
+            return 0
+
+        if count > 4:
+            lax.fori_loop(0, count, body, 0)
+        else:
+            for n in range(count):
+                body(n, 0)
+
+    def collect(got, recv_sem):
+        def body(k, _):
+            slot = lax.rem(me + k, slabs)
+            pltpu.make_async_copy(got.at[slot], got.at[slot], recv_sem.at[slot]).wait()
+            return 0
+
+        lax.fori_loop(1, slabs, body, 0)
 
     def send_feat(slot, device):
         pltpu.make_async_remote_copy(
@@ -164,7 +210,10 @@
             send_feat(lane, 2 * around(xpos, move, rows_x) + core)
     send_feat(lane, partner)
 
+    paced = 0
     for k in range(1, ring // 2 + 1):
+        send_spec(paced, pace[0])
+        paced += pace[0]
         for color in range(2):
             p, q = place[color]
             for move, far in reach:
@@ -177,8 +226,9 @@
                         if far_q >= 1:
                             along_q(color, slot, move_q)
 
-    def pass_on(k):
+    def pass_on(k, start, count):
         def body(j, _):
+            send_spec(start + j * count, count)
             m = (j + 1) // 2
             flip = 1 - 2 * lax.rem(j, 2)
             for color in range(2):
@@ -195,7 +245,8 @@
         lax.fori_loop(0, ring, body, 0)
 
     for k in range(1, ring // 2 + 1):
-        pass_on(k)
+        pass_on(k, paced, pace[k])
+        paced += ring * pace[k]
         for move, far in reach_x:
             if k <= far:
                 slot = 2 * around(xpos, -move * k, rows_x) + core
@@ -204,32 +255,13 @@
                     send_feat(slot, 2 * around(xpos, move, rows_x) + core)
                 send_feat(slot, partner)
 
-    def scatter(buffer, got, send_sem, recv_sem, low, high):
-        def body(k, _):
-            away = lax.rem(k * 29, slabs)
-            y_to = lax.rem(ypos + away // ring, ring)
-            z_to = lax.rem(zpos + lax.rem(away, ring), ring)
-            peer = y_to * ring + z_to
-            pltpu.make_async_remote_copy(
-                src_ref=buffer.at[peer], dst_ref=got.at[me], send_sem=send_sem,
-                recv_sem=recv_sem.at[me], device_id=(peer, lane), device_id_type=MESH,
-            ).start()
-            return 0
-
-        lax.fori_loop(low, high, body, 0)
-
-    def collect(got, recv_sem):
-        def body(k, _):
-            slot = lax.rem(me + k, slabs)
-            pltpu.make_async_copy(got.at[slot], got.at[slot], recv_sem.at[slot]).wait()
-            return 0
-
-        lax.fori_loop(1, slabs, body, 0)
-
-    early = slabs // 4
-    scatter(spec_out, spec_got, spec_send, spec_recv, 1, early)
-    own_spec = pltpu.make_async_copy(spec_out.at[me], spec_got.at[me], self_sem.at[0])
-    own_spec.start()
+    send_spec(paced, pace[-1])
+    own_spec = [
+        pltpu.make_async_copy(spec_out.at[g, me], spec_got.at[g, me], self_sem.at[g])
+        for g in range(2)
+    ]
+    for c in own_spec:
+        c.start()
 
     for x in range(rows_x):
         wait_feat(2 * x + 1 - core)
@@ -249,10 +281,10 @@
         cols = pl.ds(128 * j, 128)
         value = gk[:, cols].astype(F32) * acc[:, cols]
         sig_out[pl.ds(per * j, per)] = value.T.reshape(per, OWN, tok).astype(BF16)
-    scatter(sig_out, sig_got, sig_send, sig_recv, 1, slabs)
-    own_sig = pltpu.make_async_copy(sig_out.at[me], sig_got.at[me], self_sem.at[1])
+    scatter(sig_out, sig_got, sig_send, sig_recv)
+    own_sig = pltpu.make_async_copy(sig_out.at[me], sig_got.at[me], self_sem.at[2])
     own_sig.start()
-    scatter(spec_out, spec_got, spec_send, spec_recv, early, slabs)
+    send_spec(paced + pace[-1], 2 * (slabs - 1) - paced - pace[-1])
 
     for i in (6, 7, 8, 9):
         copies[i].wait()
@@ -272,10 +304,10 @@
     sin_t = turn[1]
     freqs = 2 * slabs
 
-    def go_forward(g, _):
+    def go_forward(g):
         pieces = []
-        for u in range(group):
-            x = every(sig_rows, g * group + u, slabs, OWN).astype(BF16)
+        for u in range(HALF):
+            x = every(sig_rows, g * HALF + u, slabs, OWN).astype(BF16)
             a = dot(first[...], jnp.concatenate([x, x], axis=0))
             re, im = a[:freqs], a[freqs:]
             pieces.append(
@@ -284,36 +316,30 @@
         b = jnp.concatenate(pieces, axis=0)
         b_hi = b.astype(BF16)
         b_lo = (b - b_hi.astype(F32)).astype(BF16)
-        full = dot(b_hi, mat[0]) + dot(b_hi, mat[1]) + dot(b_lo, mat[0])
-        forward[pl.ds(g * group, group)] = full.reshape(group, freqs, 2 * tok)
-        return 0
-
-    lax.fori_loop(0, OWN // group, go_forward, 0)
-
-    own_spec.wait()
-    collect(spec_got, spec_recv)
-    for j in range(2 * tok // 128):
-        spec_rows[j] = (
-            spec_got[:, :, pl.ds(128 * j, 128)].astype(F32).reshape(slabs * 2 * OWN, 128)
-        )
-
-    def go_back(g, _):
+        forward[...] = dot(b_hi, mat[0]) + dot(b_hi, mat[1]) + dot(b_lo, mat[0])
+
+    def go_back(g):
+        for j in range(tok // 128):
+            spec_rows[j] = (
+                spec_got[g, :, :, pl.ds(128 * j, 128)].astype(F32).reshape(slabs * 2 * OWN, 128)
+            )
         pieces = []
-        for u in range(group):
-            c = g * group + u
-            h = jnp.concatenate(
-                [every(spec_rows, odd * OWN + c, slabs, 2 * OWN) for odd in range(2)],
-                axis=0,
-            )
-            x = forward[c]
-            hr, hi = h[:, :tok], h[:, tok:]
+        for u in range(HALF):
+            hr, hi = (
+                jnp.concatenate(
+                    [every(spec_rows, part * OWN + b * HALF + u, slabs, 2 * OWN) for b in range(2)],
+                    axis=0,
+                )
+                for part in range(2)
+            )
+            x = forward[pl.ds(u * freqs, freqs), :]
             xr, xi = x[:, :tok], x[:, tok:]
             pieces.append(
                 jnp.concatenate([hr * xr - hi * xi, -(hr * xi + hi * xr)], axis=1).astype(BF16)
             )
         v = jnp.concatenate(pieces, axis=0)
         z = dot(v, mat[0]) + dot(v, mat[1])
-        for u in range(group):
+        for u in range(HALF):
             zr = z[u * freqs : (u + 1) * freqs, :tok]
             zi = z[u * freqs : (u + 1) * freqs, tok:]
             both = jnp.concatenate(
@@ -322,16 +348,24 @@
             y = dot(last[...], jnp.concatenate([both, both], axis=0))
             y = y * (1.0 / length)
             for j in range(tok // 128):
-                conv_rows[j, pl.ds(g * group + u, slabs, stride=OWN), :] = y[:, 128 * j : 128 * j + 128]
-        return 0
-
-    lax.fori_loop(0, OWN // group, go_back, 0)
-
-    for j in range(tok // 128):
-        ret_out[:, :, pl.ds(128 * j, 128)] = conv_rows[j].reshape(slabs, OWN, 128).astype(BF16)
-    scatter(ret_out, ret_got, ret_send, ret_recv, 1, slabs)
-    own_ret = pltpu.make_async_copy(ret_out.at[me], ret_got.at[me], self_sem.at[2])
-    own_ret.start()
+                conv_rows[j, pl.ds(u, slabs, stride=HALF), :] = y[:, 128 * j : 128 * j + 128]
+        for j in range(tok // 128):
+            ret_out[g, :, :, pl.ds(128 * j, 128)] = (
+                conv_rows[j].reshape(slabs, HALF, 128).astype(BF16)
+            )
+
+    own_ret = []
+    for g in range(2):
+        go_forward(g)
+        own_spec[g].wait()
+        collect(spec_got.at[g], spec_recv.at[g])
+        go_back(g)
+        scatter(ret_out.at[g], ret_got.at[g], ret_send.at[g], ret_recv.at[g])
+        own_ret.append(
+            pltpu.make_async_copy(ret_out.at[g, me], ret_got.at[g, me], self_sem.at[3 + g])
+        )
+        own_ret[g].start()
+
     copies[5].wait()
     pltpu.make_async_copy(
         wt.at[:, pl.ds(0, slabs - 1)], wt.at[:, pl.ds(0, slabs - 1)], wt_send
@@ -339,15 +373,21 @@
     sent = 2 * rows_x - 1
     pltpu.make_async_copy(feat.at[pl.ds(0, sent)], feat.at[pl.ds(0, sent)], feat_send).wait()
     rest = pl.ds(0, slabs - 1)
-    pltpu.make_async_copy(spec_out.at[rest], spec_out.at[rest], spec_send).wait()
+    for g in range(2):
+        pltpu.make_async_copy(spec_out.at[g, rest], spec_out.at[g, rest], spec_send.at[g]).wait()
     pltpu.make_async_copy(sig_out.at[rest], sig_out.at[rest], sig_send).wait()
-    own_ret.wait()
-    collect(ret_got, ret_recv)
+    for g in range(2):
+        own_ret[g].wait()
+        collect(ret_got.at[g], ret_recv.at[g])
     for j in range(chans // 128):
         cols = pl.ds(128 * j, 128)
-        value = ret_got[pl.ds(per * j, per)].astype(F32).reshape(128, tok).T
+        value = jnp.concatenate(
+            [ret_got[g, pl.ds(per * j, per)].astype(F32) for g in range(2)], axis=1
+        )
+        value = value.reshape(128, tok).T
         out_ref[:, cols] = (gq[:, cols].astype(F32) * value).astype(BF16)
-    pltpu.make_async_copy(ret_out.at[rest], ret_out.at[rest], ret_send).wait()
+    for g in range(2):
+        pltpu.make_async_copy(ret_out.at[g, rest], ret_out.at[g, rest], ret_send.at[g]).wait()
 
 
 def per_device(ring, rows_x, features, proj_weight, gate_q, gate_k, filter_spec):
@@ -370,33 +410,33 @@
         vm(last.shape, BF16),
         vm(turn.shape, F32),
         vm(basis.shape, BF16),
-        vm((slabs, 2 * OWN, 2 * tok), BF16),
-        vm((slabs, 2 * OWN, 2 * tok), BF16),
+        vm((2, slabs, 2 * OWN, tok), BF16),
+        vm((2, slabs, 2 * OWN, tok), BF16),
         vm((slabs, OWN, tok), BF16),
         vm((slabs, OWN, tok), BF16),
-        vm((slabs, OWN, tok), BF16),
-        vm((slabs, OWN, tok), BF16),
+        vm((2, slabs, HALF, tok), BF16),
+        vm((2, slabs, HALF, tok), BF16),
         vm((tok, chans), F32),
         vm((tok // 128, slabs * OWN, 128), F32),
-        vm((2 * tok // 128, slabs * 2 * OWN, 128), F32),
-        vm((OWN, freqs, 2 * tok), F32),
+        vm((tok // 128, slabs * 2 * OWN, 128), F32),
+        vm((HALF * freqs, 2 * tok), F32),
         vm((2, 2 * tok, 2 * tok), BF16),
-        vm((tok // 128, slabs * OWN, 128), F32),
+        vm((tok // 128, slabs * HALF, 128), F32),
         dma((10,)),
         dma,
         dma((lanes,)),
         dma,
         dma((2, slabs)),
+        dma((2,)),
+        dma((2, slabs)),
         dma,
         dma((slabs,)),
-        dma,
-        dma((slabs,)),
-        dma,
-        dma((slabs,)),
-        dma((3,)),
+        dma((2,)),
+        dma((2, slabs)),
+        dma((5,)),
     ]
     return pl.pallas_call(
-        functools.partial(kernel, ring, rows_x, tok, 4),
+        functools.partial(kernel, ring, rows_x, tok, PACE),
         out_shape=jax.ShapeDtypeStruct((tok, chans), BF16),
         in_specs=[any_space] * 9,
         out_specs=pl.BlockSpec(memory_space=pltpu.VMEM),

time: 127 us -> 113 us (0.89)
  the two profiles are of different devices: /device:TPU:16 before, /device:TPU:1 now
where the time goes in v2:
time: 113 us
  Pallas kernels  111 us (98%)
  local copies, waits for them, and re-layouts  1.77 us (2%)
    pallas_call x1, Pallas kernels, per_device(): pl.pallas_call(functools.partial(kernel, ring, rows_x, tok, PACE), out_sh...  111 us

profile of v2, /device:TPU:1, one launch (start us, length us, event | category | flops | bytes accessed | tf_op | source)
XLA Modules:
  0.0 112.9 jit_solution(3544485216138892828)
XLA Ops:
  0.0 111.2 %hyena.1 = bf16[384,512]{1,0:T(8,128)(2,1)} custom-call(bf16[384,512]{1,0:T(8,128)(2,1)} %feat_in.1, bf16[64,512]{1,0:T(8,128)(2,1)} %wt_in.1, bf16[384,512]{1,0:T(8,128)(2,1)} %gq_in.1, bf16[384,512]{1,0:T(8,128)(2,1)} %gk_in.1, f32[2,2,384,512]{3,2,1,0:T(8,128)} %spec_in.1, bf16[256,128]{1,0:T(8,128)(2,1)} %constant.8.clone.first_in, ...), custom_call_target="tpu_custom_call" | custom-call | tf_op jit(solution)/shard_map/hyena/pallas_call | solution.py:438
  111.2 1.8 %copy.11 = bf16[384,512]{1,0:T(8,128)(2,1)} copy(bf16[384,512]{1,0:T(8,128)(2,1)} %hyena.1) | data formatting | bytes 786432

commit v3 on v2

--- a/solution.py
+++ b/solution.py
@@ -13,7 +13,7 @@
 MESH = pl.DeviceIdType.MESH
 OWN = 8
 HALF = OWN // 2
-PACE = (2, 2, 2, 2, 2, 8)
+PACE = (2, 2, 2, 1, 1, 8)
 
 
 def hi_lo(table):
@@ -57,7 +57,7 @@
     spec_out, spec_got, sig_out, sig_got, ret_out, ret_got,
     acc, sig_rows, spec_rows, forward, mat, conv_rows,
     load_sem, feat_send, feat_recv, wt_send, wt_recv,
-    spec_send, spec_recv, sig_send, sig_recv, ret_send, ret_recv, self_sem,
+    spec_send, spec_recv, sig_send, sig_recv, ret_send, ret_recv, self_sem, met,
 ):
     slabs = ring * ring
     chans = acc.shape[1]
@@ -95,15 +95,21 @@
 
     barrier = pltpu.get_barrier_semaphore()
 
+    def along_z(k):
+        return ypos * ring + lax.rem(zpos + k, ring)
+
+    def along_y(k):
+        return lax.rem(ypos + k, ring) * ring + zpos
+
     def greet(k, _):
-        peer = lax.rem(me + k, slabs)
-        pl.semaphore_signal(barrier, inc=1, device_id=(peer, lane), device_id_type=MESH)
+        for peer in (along_z(k), along_y(k)):
+            pl.semaphore_signal(barrier, inc=1, device_id=(peer, lane), device_id_type=MESH)
         return 0
 
-    lax.fori_loop(1, slabs, greet, 0)
+    lax.fori_loop(1, ring, greet, 0)
     partner = 2 * xpos + 1 - core
     pl.semaphore_signal(barrier, inc=1, device_id=(me, partner), device_id_type=MESH)
-    greeted = slabs
+    greeted = 2 * (ring - 1) + 1
     if rows_x > 1:
         for move in (1, -1):
             peer = 2 * around(xpos, move, rows_x) + core
@@ -125,6 +131,12 @@
     for i in (0, 1, 2):
         copies[i].wait()
     pl.semaphore_wait(barrier, greeted)
+
+    def tell(k, _):
+        pl.semaphore_signal(met, inc=1, device_id=(along_z(k), lane), device_id_type=MESH)
+        return 0
+
+    lax.fori_loop(1, ring, tell, 0)
 
     def send_to(k, buffer, got, send_sem, recv_sem):
         away = lax.rem(k * 29, slabs)
@@ -210,6 +222,7 @@
             send_feat(lane, 2 * around(xpos, move, rows_x) + core)
     send_feat(lane, partner)
 
+    pl.semaphore_wait(met, ring - 1)
     paced = 0
     for k in range(1, ring // 2 + 1):
         send_spec(paced, pace[0])
@@ -244,7 +257,25 @@
 
         lax.fori_loop(0, ring, body, 0)
 
+    per_feat = feat.shape[2] // wt.shape[2]
+    last_row = around(ypos, -step_a * (ring // 2), ring)
+
+    def project(color, low, count):
+        def body(n, _):
+            f = lax.rem(low + n, 2 * rows_x)
+            block = wt[color, pl.ds(f * per_feat, per_feat)].reshape(feat.shape[2], half)
+            acc[:, pl.ds(color * half, half)] += dot(feat[f], block)
+            return 0
+
+        lax.fori_loop(0, count, body, 0)
+
     for k in range(1, ring // 2 + 1):
+        if k == ring // 2:
+            for x in range(rows_x):
+                wait_feat(2 * x + 1 - core)
+            acc[...] = jnp.zeros_like(acc)
+            copies[4].wait()
+            project(0, last_row + 1, 2 * rows_x - 1)
         pass_on(k, paced, pace[k])
         paced += ring * pace[k]
         for move, far in reach_x:
@@ -263,20 +294,8 @@
     for c in own_spec:
         c.start()
 
-    for x in range(rows_x):
-        wait_feat(2 * x + 1 - core)
-
-    copies[4].wait()
-    acc[...] = jnp.zeros_like(acc)
-    per_feat = feat.shape[2] // wt.shape[2]
-
-    def project(f, _):
-        for color in range(2):
-            block = wt[color, pl.ds(f * per_feat, per_feat)].reshape(feat.shape[2], half)
-            acc[:, pl.ds(color * half, half)] += dot(feat[f], block)
-        return 0
-
-    lax.fori_loop(0, 2 * rows_x, project, 0)
+    project(0, last_row, 1)
+    project(1, 0, 2 * rows_x)
     for j in range(chans // 128):
         cols = pl.ds(128 * j, 128)
         value = gk[:, cols].astype(F32) * acc[:, cols]
@@ -434,6 +453,7 @@
         dma((2,)),
         dma((2, slabs)),
         dma((5,)),
+        pltpu.SemaphoreType.REGULAR,
     ]
     return pl.pallas_call(
         functools.partial(kernel, ring, rows_x, tok, PACE),

time: 113 us -> 109 us (0.965)
  Pallas kernels: 111 us -> 107 us
    pallas_call x1, Pallas kernels: 111 us -> 107 us  [per_device(): pl.pallas_call(functools.partial(kernel, ring, rows_x, tok, PACE), out_sh...]
where the time goes in v3:
time: 109 us
  Pallas kernels  107 us (98%)
  local copies, waits for them, and re-layouts  1.77 us (2%)
    pallas_call x1, Pallas kernels, per_device(): pl.pallas_call(functools.partial(kernel, ring, rows_x, tok, PACE), out_sh...  107 us

profile of v3, /device:TPU:1, one launch (start us, length us, event | category | flops | bytes accessed | tf_op | source)
XLA Modules:
  0.0 109.1 jit_solution(9121177485378439391)
XLA Ops:
  0.0 107.4 %hyena.1 = bf16[384,512]{1,0:T(8,128)(2,1)} custom-call(bf16[384,512]{1,0:T(8,128)(2,1)} %feat_in.1, bf16[64,512]{1,0:T(8,128)(2,1)} %wt_in.1, bf16[384,512]{1,0:T(8,128)(2,1)} %gq_in.1, bf16[384,512]{1,0:T(8,128)(2,1)} %gk_in.1, f32[2,2,384,512]{3,2,1,0:T(8,128)} %spec_in.1, bf16[256,128]{1,0:T(8,128)(2,1)} %constant.8.clone.first_in, ...), custom_call_target="tpu_custom_call" | custom-call | tf_op jit(solution)/shard_map/hyena/pallas_call | solution.py:458
  107.4 1.8 %copy.11 = bf16[384,512]{1,0:T(8,128)(2,1)} copy(bf16[384,512]{1,0:T(8,128)(2,1)} %hyena.1) | data formatting | bytes 786432

commit v4 on v3

--- a/solution.py
+++ b/solution.py
@@ -78,8 +78,8 @@
         return q * ring + p if color == 0 else p * ring + q
 
     loads = [
-        (wt_in.at[:, pl.ds(0, half)], wt.at[0, me]),
-        (wt_in.at[:, pl.ds(half, half)], wt.at[1, me]),
+        (wt_in.at[:, pl.ds(0, half)], wt.at[0, ypos * ring + zpos]),
+        (wt_in.at[:, pl.ds(half, half)], wt.at[1, zpos * ring + ypos]),
         (feat_in, feat.at[lane]),
         (spec_in, spec),
         (gk_in, gk),
@@ -211,11 +211,11 @@
     for color in range(2):
         for move, far in reach:
             if far >= 1:
-                along_p(color, me, move)
+                along_p(color, place[color][1] * ring + place[color][0], move)
     for color in range(2):
         for move, far in reach:
             if far >= 1:
-                along_q(color, me, move)
+                along_q(color, place[color][1] * ring + place[color][0], move)
     reach_x = ((step_a, rows_x // 2), (-step_a, rows_x // 2 - 1))
     for move, far in reach_x:
         if far >= 1:
@@ -231,7 +231,7 @@
             p, q = place[color]
             for move, far in reach:
                 if k <= far:
-                    slot = spot(color, around(p, -move * k, ring), q)
+                    slot = q * ring + around(p, -move * k, ring)
                     wait_wt(color, slot)
                     if k < far:
                         along_p(color, slot, move)
@@ -239,23 +239,35 @@
                         if far_q >= 1:
                             along_q(color, slot, move_q)
 
+    def pair(color, low):
+        return wt.at[color, pl.ds(low, 2)]
+
     def pass_on(k, start, count):
         def body(j, _):
-            send_spec(start + j * count, count)
-            m = (j + 1) // 2
-            flip = 1 - 2 * lax.rem(j, 2)
+            send_spec(start + j * 2 * count, 2 * count)
             for color in range(2):
                 p, q = place[color]
-                from_p = around(p, flip * step_a * m, ring)
+                first_p = 2 * lax.rem(p // 2 + j, ring // 2)
                 for move, far in reach:
                     if k <= far:
-                        slot = spot(color, from_p, around(q, -move * k, ring))
-                        wait_wt(color, slot)
+                        low = around(q, -move * k, ring) * ring + first_p
+                        if k == 1:
+                            wait_wt(color, low)
+                            wait_wt(color, low + 1)
+                        else:
+                            pltpu.make_async_copy(
+                                pair(color, low), pair(color, low), wt_recv.at[color, low]
+                            ).wait()
                         if k < far:
-                            along_q(color, slot, move)
+                            pltpu.make_async_remote_copy(
+                                src_ref=pair(color, low), dst_ref=pair(color, low),
+                                send_sem=wt_send, recv_sem=wt_recv.at[color, low],
+                                device_id=(spot(color, p, around(q, move, ring)), lane),
+                                device_id_type=MESH,
+                            ).start()
             return 0
 
-        lax.fori_loop(0, ring, body, 0)
+        lax.fori_loop(0, ring // 2, body, 0)
 
     per_feat = feat.shape[2] // wt.shape[2]
     last_row = around(ypos, -step_a * (ring // 2), ring)
@@ -263,7 +275,10 @@
     def project(color, low, count):
         def body(n, _):
             f = lax.rem(low + n, 2 * rows_x)
-            block = wt[color, pl.ds(f * per_feat, per_feat)].reshape(feat.shape[2], half)
+            if color == 0:
+                block = wt[0, pl.ds(f * per_feat, per_feat)].reshape(feat.shape[2], half)
+            else:
+                block = jnp.concatenate([wt[1, z * ring + f] for z in range(ring)], axis=0)
             acc[:, pl.ds(color * half, half)] += dot(feat[f], block)
             return 0
 

time: 109 us -> 110 us (level)
  no operation moved by 1% of the time
where the time goes in v4:
time: 110 us; the launch traced here: 109 us
  Pallas kernels  108 us (98%)
  local copies, waits for them, and re-layouts  1.77 us (2%)
    pallas_call x1, Pallas kernels, per_device(): pl.pallas_call(functools.partial(kernel, ring, rows_x, tok, PACE), out_sh...  108 us

profile of v4, /device:TPU:1, one launch (start us, length us, event | category | flops | bytes accessed | tf_op | source)
XLA Modules:
  0.0 109.3 jit_solution(17977754452046520996)
XLA Ops:
  0.0 107.5 %hyena.1 = bf16[384,512]{1,0:T(8,128)(2,1)} custom-call(bf16[384,512]{1,0:T(8,128)(2,1)} %feat_in.1, bf16[64,512]{1,0:T(8,128)(2,1)} %wt_in.1, bf16[384,512]{1,0:T(8,128)(2,1)} %gq_in.1, bf16[384,512]{1,0:T(8,128)(2,1)} %gk_in.1, f32[2,2,384,512]{3,2,1,0:T(8,128)} %spec_in.1, bf16[256,128]{1,0:T(8,128)(2,1)} %constant.8.clone.first_in, ...), custom_call_target="tpu_custom_call" | custom-call | tf_op jit(solution)/shard_map/hyena/pallas_call | solution.py:473
  107.5 1.8 %copy.11 = bf16[384,512]{1,0:T(8,128)(2,1)} copy(bf16[384,512]{1,0:T(8,128)(2,1)} %hyena.1) | data formatting | bytes 786432
